TPU v7x, 32 devices: a whole 2x2x4 slice. The times are simulated.
32 devices in a mesh: grp: 2 (over y), gx: 4 (over x, core), gy: 4 (over z).
Axes of the slice: x: 2, y: 2, z: 4, core: 2. Of those that a mesh axis runs over, the one named last changes fastest.
Arguments:
- ensemble: float32 [128, 3, 32, 1024], P('grp', None, 'gx', 'gy'), parts along dimension 0, may hold values from -16 to 16
- diffusivity: float32 [6, 32, 1024], P('grp', 'gx', 'gy'), parts along dimension 0, may hold values from 0.03 to 0.24
- mixing: float32 [3, 3], replicated, may hold values from -0.6 to 0.6
- obs_cell: int32 [4, 4, 4096], P('gx', 'gy', 'grp'), parts along dimension 2, may hold values from 0 to 2047
- obs_var: int32 [4, 4, 4096], P('gx', 'gy', 'grp'), parts along dimension 2, may hold values from 0 to 2
- obs_value: float32 [4, 4, 4096], P('gx', 'gy', 'grp'), parts along dimension 2, may hold values from -5 to 5
- obs_weight: float32 [4, 4, 4096], P('gx', 'gy', 'grp'), parts along dimension 2, may hold values from 0.5 to 6
Outputs:
- analysis: float32 [128, 3, 32, 1024], P('grp', None, 'gx', 'gy'), parts along dimension 0
There are 2 independent parts, one for each index of `grp`. A program takes and returns all parts, laid end to end along the dimension named above; an argument that names none is the same for every part. Nothing has to cross between parts.
All inputs are finite; a program needn't handle non-finite values.
Results may differ from a plain program's by a relative error of at most 0.0001.
Values sent between devices are 32-bit elements; how exact they have to be, the bound alone decides.
No kernel may reach another device: no remote copies, remote signals or barrier semaphores. Data moves between devices by JAX's collectives and lax.ppermute only.
A program may use at most 64 MiB of HBM per device.

v0:
```python
import math
import jax
import jax.numpy as jnp
from jax import lax
from jax.sharding import PartitionSpec as P

NS_ITERS = 5


def padded_2(cells, sides, width):
    for axis, dim in sides:
        count = lax.axis_size(axis)
        ends = count - 1
        head = lax.slice_in_dim(cells, 0, width, axis=dim)
        tail = lax.slice_in_dim(cells, cells.shape[dim] - width, cells.shape[dim], axis=dim)
        cells = jnp.concatenate(
            [
                lax.ppermute(tail, axis, [(i, (i + 1) % count) for i in range(ends)]),
                cells,
                lax.ppermute(head, axis, [((i + 1) % count, i) for i in range(ends)]),
            ],
            axis=dim,
        )
    return cells


def advance(padded, kappa_field, mixing):
    center = padded[:, :, 1:-1, 1:-1]
    beside = padded[:, :, 2:, 1:-1] + padded[:, :, :-2, 1:-1]
    beside = beside + padded[:, :, 1:-1, 2:] + padded[:, :, 1:-1, :-2]
    coupled = jnp.zeros_like(center)
    for source in range(3):
        coupled = coupled + mixing[:, source][None, :, None, None] * center[:, source][:, None]
    return center + kappa_field[None] * (beside - 4.0 * center) + coupled


def pad_faces(state):
    return padded_2(state, (("gx", 2), ("gy", 3)), 1)


def transform(gram, pull):
    identity = jnp.eye(gram.shape[0], dtype=jnp.float32)
    matrix = identity + gram
    frob_norm = jnp.sqrt(jnp.sum(matrix * matrix))

    def ns_step(step, carry):
        sqrt_iter, inv_iter = carry
        correction = 1.5 * identity - 0.5 * jnp.dot(
            inv_iter, sqrt_iter, precision=lax.Precision.HIGHEST
        )
        return (
            jnp.dot(sqrt_iter, correction, precision=lax.Precision.HIGHEST),
            jnp.dot(correction, inv_iter, precision=lax.Precision.HIGHEST),
        )

    sqrt_iter, inv_iter = lax.fori_loop(0, NS_ITERS, ns_step, (matrix / frob_norm, identity))
    root_inv = inv_iter / jnp.sqrt(frob_norm)
    inverse = jnp.dot(root_inv, root_inv, precision=lax.Precision.HIGHEST)
    mean_shift = jnp.dot(inverse, pull, precision=lax.Precision.HIGHEST)
    return mean_shift[:, None] + root_inv


def local(ensemble, diffusivity, mixing, obs_cell, obs_var, obs_value, obs_weight):
    members = ensemble.shape[0]
    first_state = advance(pad_faces(ensemble), diffusivity, mixing)
    second_state = advance(pad_faces(first_state), diffusivity, mixing)
    cell_count = second_state.shape[2] * second_state.shape[3]
    flat_state = second_state.reshape(members, -1)
    obs_index = obs_var[0, 0] * cell_count + obs_cell[0, 0]
    observed = jnp.take(flat_state, obs_index, axis=1)
    obs_mean = jnp.mean(observed, axis=0)
    obs_total = obs_cell.shape[2] * lax.axis_size("gx") * lax.axis_size("gy")
    factor = 1.0 / math.sqrt((members - 1) * obs_total)
    weight = obs_weight[0, 0]
    spread = (observed - obs_mean) * (weight * factor)
    departure = weight * (obs_value[0, 0] - obs_mean)
    gram_part = jnp.dot(spread, spread.T, precision=lax.Precision.HIGHEST)
    pull_part = jnp.dot(spread, departure, precision=lax.Precision.HIGHEST)
    gram, pull = lax.psum((gram_part, pull_part), ("gx", "gy"))
    state_mean = jnp.mean(second_state, axis=0)
    anomalies = (second_state - state_mean).reshape(members, -1)
    weights = transform(gram, pull)
    moved = jnp.dot(weights.T, anomalies, precision=lax.Precision.HIGHEST)
    return state_mean + moved.reshape(second_state.shape)


def solution(mesh):
    return jax.shard_map(
        local,
        mesh=mesh,
        in_specs=(
            P("grp", None, "gx", "gy"),
            P("grp", "gx", "gy"),
            P(),
            P("gx", "gy", "grp"),
            P("gx", "gy", "grp"),
            P("gx", "gy", "grp"),
            P("gx", "gy", "grp"),
        ),
        out_specs=P("grp", None, "gx", "gy"),
        check_vma=False,
    )
```

profile of v0, /device:TPU:2, one launch (start us, length us, event | category | flops | bytes accessed | tf_op | source)
XLA Modules:
  0.0 147.9 jit_solution(570074319774280910)
XLA Ops:
  0.0 2.0 %copy.48 = f32[64,3,8,256]{3,0,2,1:T(8,128)S(1)} copy(f32[64,3,8,256]{3,2,1,0:T(8,128)} %param.9) | data formatting | bytes 3145728 | tf_op args[0]
  2.1 1.9 %collective-permute-start.1 = (f32[64,3,1,256]{3,0,2,1:T(8,128)S(1)}, f32[64,3,1,256]{3,0,2,1:T(8,128)S(1)}, u32[]{:S(2)}, u32[]{:S(2)}) collective-permute-start(f32[64,3,1,256]{3,0,2,1:T(8,128)S(1)} %get-tuple-element.73), channel_id=1, source_target_pairs={{0,4},{4,8},{8,12},{1,5},{5,9},{9,13},{2,6},{6,10},{10,14},{3,7},{... | collective-permute-start | bytes 589832 | tf_op jit(solution)/shard_map/ppermute | solution.py:18
  4.0 3.6 %collective-permute-start = (f32[64,3,1,256]{3,0,2,1:T(8,128)S(1)}, f32[64,3,1,256]{3,0,2,1:T(8,128)S(1)}, u32[]{:S(2)}, u32[]{:S(2)}) collective-permute-start(f32[64,3,1,256]{3,0,2,1:T(8,128)S(1)} %get-tuple-element.72), channel_id=1, source_target_pairs={{4,0},{8,4},{12,8},{5,1},{9,5},{13,9},{6,2},{10,6},{14,10},{7,3},{... | collective-permute-start | bytes 589832 | tf_op jit(solution)/shard_map/ppermute | solution.py:20
  7.7 1.1 slice_bitcast_fusion.5
  8.8 0.6 fusion.34
  9.5 0.5 constant_dynamic-update-slice_fusion.1
  10.1 0.7 collective-permute-done
  10.9 1.3 fusion.44
  12.2 1.6 %copy.43 = f32[64,3,10,1]{0,3,2,1:T(1,128)S(1)} copy(f32[64,3,10,1]{3,0,2,1:T(8,128)} %get-tuple-element.62) | data formatting | bytes 15360 | tf_op jit(solution)/shard_map/slice | solution.py:14
  13.7 1.3 collective-permute-start.2
  15.0 0.3 copy.45
  15.4 4.6 %collective-permute-start.3 = (f32[64,3,10,1]{0,3,2,1:T(1,128)S(1)}, f32[64,3,10,1]{0,3,2,1:T(1,128)S(1)}, u32[]{:S(2)}, u32[]{:S(2)}) collective-permute-start(f32[64,3,10,1]{0,3,2,1:T(1,128)S(1)} %copy.45), channel_id=1, source_target_pairs={{0,1},{1,2},{2,3},{4,5},{5,6},{6,7},{8,9},{9,10},{10,11},{12,13},{... | collective-permute-start | bytes 23048 | tf_op jit(solution)/shard_map/ppermute | solution.py:18
  20.0 0.7 slice_reduce_fusion.2
  20.7 2.0 %copy.49 = f32[64,8,256]{2,0,1:T(8,128)} copy(f32[64,8,256]{2,1,0:T(8,128)} %get-tuple-element.69) | data formatting | bytes 1048576 | tf_op jit(solution)/shard_map/mul | solution.py:33
  22.7 2.0 %copy.50 = f32[64,8,256]{2,0,1:T(8,128)} copy(f32[64,8,256]{2,1,0:T(8,128)} %get-tuple-element.71) | data formatting | bytes 1048576 | tf_op jit(solution)/shard_map/mul | solution.py:33
  24.7 1.0 copy.51
  25.7 1.4 copy.44
  27.1 1.3 copy.46
  28.4 5.0 %fusion.14 = f32[64,3,8,256]{3,0,2,1:T(8,128)S(1)} fusion(f32[64,3,8,256]{3,0,2,1:T(8,128)} %copy-done.2, f32[64,3,10,256]{3,0,2,1:T(8,128)S(1)} %constant_dynamic-update-slice_fusion, f32[64,3,10,1]{3,0,2,1:T(8,128)} %copy.46, f32[64,3,10,1]{3,0,2,1:T(8,128)} %copy.44, f32[64,3,1,256]{3,0,2,1:T(8,128)} %copy-done.5, f32[64,3,1,256]{3,0,2,1:T(8,128)} %copy-done.6, ...), kind=kLoop, calls=%fused_computation.27 | loop fusion | flops 6684672 | bytes 7117860 | tf_op jit(solution)/shard_map/add | solution.py:34
  33.4 3.3 %collective-permute-start.4 = (f32[64,3,1,256]{3,0,2,1:T(8,128)S(1)}, f32[64,3,1,256]{3,0,2,1:T(8,128)S(1)}, u32[]{:S(2)}, u32[]{:S(2)}) collective-permute-start(f32[64,3,1,256]{3,0,2,1:T(8,128)S(1)} %get-tuple-element.65), channel_id=1, source_target_pairs={{4,0},{8,4},{12,8},{5,1},{9,5},{13,9},{6,2},{10,6},{14,10},{7,3},{... | collective-permute-start | bytes 589832 | tf_op jit(solution)/shard_map/ppermute | solution.py:20
  36.7 1.9 %collective-permute-start.5 = (f32[64,3,1,256]{3,0,2,1:T(8,128)S(1)}, f32[64,3,1,256]{3,0,2,1:T(8,128)S(1)}, u32[]{:S(2)}, u32[]{:S(2)}) collective-permute-start(f32[64,3,1,256]{3,0,2,1:T(8,128)S(1)} %get-tuple-element.64), channel_id=1, source_target_pairs={{0,4},{4,8},{8,12},{1,5},{5,9},{9,13},{2,6},{6,10},{10,14},{3,7},{... | collective-permute-start | bytes 589832 | tf_op jit(solution)/shard_map/ppermute | solution.py:18
  38.6 0.6 compare_and_fusion
  39.2 0.7 collective-permute-done.4
  39.9 3.8 %collective-permute-done.5 = f32[64,3,1,256]{3,0,2,1:T(8,128)S(1)} collective-permute-done((f32[64,3,1,256]{3,0,2,1:T(8,128)S(1)}, f32[64,3,1,256]{3,0,2,1:T(8,128)S(1)}, u32[]{:S(2)}, u32[]{:S(2)}) %collective-permute-start.5) | collective-permute-done | bytes 196640 | tf_op jit(solution)/shard_map/ppermute | solution.py:18
  43.8 0.5 copy-done.8
  44.3 0.4 fusion.43
  44.7 1.0 copy.52
  45.7 1.3 collective-permute-start.6
  47.0 0.3 copy.54
  47.3 5.2 %collective-permute-start.7 = (f32[64,3,10,1]{0,3,2,1:T(1,128)S(1)}, f32[64,3,10,1]{0,3,2,1:T(1,128)}, u32[]{:S(2)}, u32[]{:S(2)}) collective-permute-start(f32[64,3,10,1]{0,3,2,1:T(1,128)S(1)} %copy.54), channel_id=1, source_target_pairs={{0,1},{1,2},{2,3},{4,5},{5,6},{6,7},{8,9},{9,10},{10,11},{12,13},{... | collective-permute-start | bytes 23048 | tf_op jit(solution)/shard_map/ppermute | solution.py:18
  52.4 1.2 slice_bitcast_fusion.2
  53.7 0.4 copy.53
  54.0 1.1 copy.55
  55.2 4.6 %fusion.41 = (f32[3,8,256]{2,1,0:T(8,128)}, f32[64,3,8,256]{3,0,2,1:T(8,128)}) fusion(f32[64,8,256]{2,0,1:T(8,128)} %get-tuple-element.68, f32[3]{0:T(128)S(1)} %copy-done.17, f32[64,8,256]{2,0,1:T(8,128)} %get-tuple-element.67, f32[3]{0:T(128)} %get-tuple-element.47, f32[64,8,256]{2,0,1:T(8,128)} %get-tuple-element.66, f32[3]{0:T(128)S(1)} %copy-done.16, ...), kind=kLoop, calls=%fused_computation.85 | loop fusion | flops 8644608 | bytes 5176356 | tf_op jit(solution)/shard_map/reduce_sum | solution.py:80
  59.8 2.1 %copy.64 = f32[64,3,8,256]{0,3,2,1:T(8,128)S(1)} copy(f32[64,3,8,256]{3,0,2,1:T(8,128)} %get-tuple-element.59) | data formatting | bytes 3145728 | tf_op jit(solution)/shard_map/reshape | solution.py:68
  61.9 7.6 %gather_fusion = f32[2048,64]{1,0:T(8,128)} fusion(f32[64,6144]{0,1:T(8,128)S(1)} %bitcast.68, s32[2048]{0:T(1024)S(1)} %broadcast_clamp_fusion), kind=kCustom, calls=%fused_computation | custom fusion | bytes 1056768 | tf_op jit(solution)/shard_map/jit(_take)/gather | solution.py:70
  69.6 1.9 %select_reduce_fusion = f32[2048]{0:T(1024)S(1)} fusion(f32[2048,64]{1,0:T(8,128)} %gather_fusion, pred[2048]{0:T(1024)(128)(4,1)S(1)} %copy-done.11), kind=kLoop, calls=%fused_computation.40 | loop fusion | flops 260096 | bytes 534528 | tf_op jit(solution)/shard_map/reduce_sum | solution.py:71
  71.6 5.4 %fusion.23 = f32[64,64]{1,0:T(8,128)S(1)} fusion(f32[2048,64]{1,0:T(8,128)} %gather_fusion, f32[2048]{0:T(1024)S(1)} %get-tuple-element.76, f32[2048]{0:T(1024)S(1)} %get-tuple-element.75, pred[2048]{0:T(1024)(128)(4,1)S(1)} %copy-done.11), kind=kOutput, calls=%fused_computation.41 | convolution fusion | flops 101056512 | bytes 559104 | tf_op jit(solution)/shard_map/dot_general | solution.py:77
  77.0 1.3 convolution_bitcast_fusion.1
  78.3 59.5 %all-reduce = (f32[64,64]{1,0:T(8,128)S(1)}, f32[64]{0:T(128)S(1)}) all-reduce(f32[64,64]{1,0:T(8,128)S(1)} %fusion.23, f32[64]{0:T(128)S(1)} %convolution_bitcast_fusion.1), channel_id=1, replica_groups=mesh['grp'=2,'gx'=4,'gy'=4] {'gx','gy'}, use_global_device_ids=true, to_apply=%region_2.3 | all-reduce | flops 4160 | bytes 33280 | tf_op jit(solution)/shard_map/psum | solution.py:79
  137.9 0.6 multiply_reduce_fusion
  139.2 3.2 %while.13 = (s32[]{:T(128)}, f32[64,64]{0,1:T(8,128)S(1)}, f32[64,64]{1,0:T(8,128)S(1)}, s32[]{:T(128)}) while((s32[]{:T(128)}, f32[64,64]{0,1:T(8,128)S(1)}, f32[64,64]{1,0:T(8,128)S(1)}, s32[]{:T(128)}) %tuple.41), condition=%wide.region_5.6_spmd.clone, body=%wide.region_4.5_spmd.clone.sunk | while | flops 9453570 | bytes 213045 | solution.py:56
  139.6 0.2 convolution_bitcast_fusion.4
  140.3 0.2 convolution_bitcast_fusion.4
  140.9 0.2 convolution_bitcast_fusion.4
  142.6 0.9 copy.68
  143.9 2.0 %fusion.19 = f32[64,3,8,256]{3,0,2,1:T(8,128)S(1)} fusion(f32[3,8,256,64]{2,1,0,3:T(8,128)S(1)} %bitcast.69, f32[3,8,256]{2,1,0:T(8,128)S(1)} %broadcast_multiply_fusion, f32[64]{0:T(128)S(1)} %convolution_bitcast_fusion.2, f32[64,64]{1,0:T(8,128)S(1)} %get-tuple-element.27, f32[]{:T(128)S(6)} %sqrt.7), kind=kOutput, calls=%fused_computation.35 | convolution fusion | flops 302391296 | bytes 3186948 | tf_op jit(solution)/shard_map/dot_general | solution.py:83
  145.8 2.1 %copy.62 = f32[64,3,8,256]{3,2,1,0:T(8,128)} copy(f32[64,3,8,256]{3,0,2,1:T(8,128)S(1)} %fusion.19) | data formatting | bytes 3145728 | tf_op jit(solution)/shard_map/add | solution.py:84
  (76 shorter events, 3.3 us)
Async XLA Ops:
  0.0 7.7 %copy-start = (f32[64,3,8,256]{3,2,1,0:T(8,128)S(1)}, f32[64,3,8,256]{3,2,1,0:T(8,128)}, u32[]{:S(2)}) copy-start(f32[64,3,8,256]{3,2,1,0:T(8,128)} %param.9) | copy-start | bytes 4718596
  2.0 6.8 %copy-start.2 = (f32[64,3,8,256]{3,0,2,1:T(8,128)}, f32[64,3,8,256]{3,0,2,1:T(8,128)S(1)}, u32[]{:S(2)}) copy-start(f32[64,3,8,256]{3,0,2,1:T(8,128)S(1)} %copy.48) | copy-start | bytes 4718596
  2.1 7.4 %collective-permute-start.1 = (f32[64,3,1,256]{3,0,2,1:T(8,128)S(1)}, f32[64,3,1,256]{3,0,2,1:T(8,128)S(1)}, u32[]{:S(2)}, u32[]{:S(2)}) collective-permute-start(f32[64,3,1,256]{3,0,2,1:T(8,128)S(1)} %get-tuple-element.73), channel_id=1, source_target_pairs={{0,4},{4,8},{8,12},{1,5},{5,9},{9,13},{2,6},{6,10},{10,14},{3,7},{... | collective-permute-start | bytes 589832 | tf_op jit(solution)/shard_map/ppermute | solution.py:18
  4.0 5.4 %copy-start.12 = (s32[1,1,2048]{2,1,0:T(1,128)S(1)}, s32[1,1,2048]{2,1,0:T(1,128)}, u32[]{:S(2)}) copy-start(s32[1,1,2048]{2,1,0:T(1,128)} %param.12) | copy-start | bytes 24580
  4.0 5.4 %copy-start.13 = (s32[1,1,2048]{2,1,0:T(1,128)S(1)}, s32[1,1,2048]{2,1,0:T(1,128)}, u32[]{:S(2)}) copy-start(s32[1,1,2048]{2,1,0:T(1,128)} %param.13) | copy-start | bytes 24580
  4.0 6.8 %collective-permute-start = (f32[64,3,1,256]{3,0,2,1:T(8,128)S(1)}, f32[64,3,1,256]{3,0,2,1:T(8,128)S(1)}, u32[]{:S(2)}, u32[]{:S(2)}) collective-permute-start(f32[64,3,1,256]{3,0,2,1:T(8,128)S(1)} %get-tuple-element.72), channel_id=1, source_target_pairs={{4,0},{8,4},{12,8},{5,1},{9,5},{13,9},{6,2},{10,6},{14,10},{7,3},{... | collective-permute-start | bytes 589832 | tf_op jit(solution)/shard_map/ppermute | solution.py:20
  9.5 0.7 copy-start.5
  10.9 1.3 copy-start.6
  12.2 7.8 %copy-start.10 = (f32[3,3]{1,0:T(4,128)S(1)}, f32[3,3]{1,0:T(4,128)}, u32[]{:S(2)}) copy-start(f32[3,3]{1,0:T(4,128)} %param.11) | copy-start | bytes 112
  13.7 12.0 %collective-permute-start.2 = (f32[64,3,10,1]{0,3,2,1:T(1,128)S(1)}, f32[64,3,10,1]{0,3,2,1:T(1,128)S(1)}, u32[]{:S(2)}, u32[]{:S(2)}) collective-permute-start(f32[64,3,10,1]{0,3,2,1:T(1,128)S(1)} %copy.43), channel_id=1, source_target_pairs={{1,0},{2,1},{3,2},{5,4},{6,5},{7,6},{9,8},{10,9},{11,10},{13,12},{... | collective-permute-start | bytes 23048 | tf_op jit(solution)/shard_map/ppermute | solution.py:20
  15.4 11.7 %collective-permute-start.3 = (f32[64,3,10,1]{0,3,2,1:T(1,128)S(1)}, f32[64,3,10,1]{0,3,2,1:T(1,128)S(1)}, u32[]{:S(2)}, u32[]{:S(2)}) collective-permute-start(f32[64,3,10,1]{0,3,2,1:T(1,128)S(1)} %copy.45), channel_id=1, source_target_pairs={{0,1},{1,2},{2,3},{4,5},{5,6},{6,7},{8,9},{9,10},{10,11},{12,13},{... | collective-permute-start | bytes 23048 | tf_op jit(solution)/shard_map/ppermute | solution.py:18
  33.4 6.4 %collective-permute-start.4 = (f32[64,3,1,256]{3,0,2,1:T(8,128)S(1)}, f32[64,3,1,256]{3,0,2,1:T(8,128)S(1)}, u32[]{:S(2)}, u32[]{:S(2)}) collective-permute-start(f32[64,3,1,256]{3,0,2,1:T(8,128)S(1)} %get-tuple-element.65), channel_id=1, source_target_pairs={{4,0},{8,4},{12,8},{5,1},{9,5},{13,9},{6,2},{10,6},{14,10},{7,3},{... | collective-permute-start | bytes 589832 | tf_op jit(solution)/shard_map/ppermute | solution.py:20
  36.7 7.0 %collective-permute-start.5 = (f32[64,3,1,256]{3,0,2,1:T(8,128)S(1)}, f32[64,3,1,256]{3,0,2,1:T(8,128)S(1)}, u32[]{:S(2)}, u32[]{:S(2)}) collective-permute-start(f32[64,3,1,256]{3,0,2,1:T(8,128)S(1)} %get-tuple-element.64), channel_id=1, source_target_pairs={{0,4},{4,8},{8,12},{1,5},{5,9},{9,13},{2,6},{6,10},{10,14},{3,7},{... | collective-permute-start | bytes 589832 | tf_op jit(solution)/shard_map/ppermute | solution.py:18
  39.9 4.0 %copy-start.7 = (f32[64,3,1,256]{3,0,2,1:T(8,128)}, f32[64,3,1,256]{3,0,2,1:T(8,128)S(1)}, u32[]{:S(2)}) copy-start(f32[64,3,1,256]{3,0,2,1:T(8,128)S(1)} %collective-permute-done.4) | copy-start | bytes 589828
  43.7 0.7 copy-start.8
  45.7 8.0 %collective-permute-start.6 = (f32[64,3,10,1]{0,3,2,1:T(1,128)}, f32[64,3,10,1]{0,3,2,1:T(1,128)S(1)}, u32[]{:S(2)}, u32[]{:S(2)}) collective-permute-start(f32[64,3,10,1]{0,3,2,1:T(1,128)} %copy.52), channel_id=1, source_target_pairs={{1,0},{2,1},{3,2},{5,4},{6,5},{7,6},{9,8},{10,9},{11,10},{13,12},{... | collective-permute-start | bytes 23048 | tf_op jit(solution)/shard_map/ppermute | solution.py:20
  47.3 6.7 %collective-permute-start.7 = (f32[64,3,10,1]{0,3,2,1:T(1,128)S(1)}, f32[64,3,10,1]{0,3,2,1:T(1,128)}, u32[]{:S(2)}, u32[]{:S(2)}) collective-permute-start(f32[64,3,10,1]{0,3,2,1:T(1,128)S(1)} %copy.54), channel_id=1, source_target_pairs={{0,1},{1,2},{2,3},{4,5},{5,6},{6,7},{8,9},{9,10},{10,11},{12,13},{... | collective-permute-start | bytes 23048 | tf_op jit(solution)/shard_map/ppermute | solution.py:18
  53.6 1.5 %copy-start.16 = (f32[3]{0:T(128)S(1)}, f32[3]{0:T(128)}, u32[]{:S(2)}) copy-start(f32[3]{0:T(128)} %get-tuple-element.45) | copy-start | bytes 40
  53.6 1.5 %copy-start.17 = (f32[3]{0:T(128)S(1)}, f32[3]{0:T(128)}, u32[]{:S(2)}) copy-start(f32[3]{0:T(128)} %get-tuple-element.46) | copy-start | bytes 40
  61.9 7.7 %copy-start.11 = (pred[2048]{0:T(1024)(128)(4,1)S(1)}, pred[2048]{0:T(1024)(128)(4,1)}, u32[]{:S(2)}) copy-start(pred[2048]{0:T(1024)(128)(4,1)} %compare_and_fusion) | copy-start | bytes 6148
  61.9 9.6 %copy-start.14 = (f32[1,1,2048]{2,1,0:T(1,128)S(1)}, f32[1,1,2048]{2,1,0:T(1,128)}, u32[]{:S(2)}) copy-start(f32[1,1,2048]{2,1,0:T(1,128)} %param.15) | copy-start | bytes 24580
  61.9 9.6 %copy-start.15 = (f32[1,1,2048]{2,1,0:T(1,128)S(1)}, f32[1,1,2048]{2,1,0:T(1,128)}, u32[]{:S(2)}) copy-start(f32[1,1,2048]{2,1,0:T(1,128)} %param.14) | copy-start | bytes 24580
  69.6 7.4 %copy-start.3 = (f32[2048,64]{1,0:T(8,128)S(1)}, f32[2048,64]{1,0:T(8,128)}, u32[]{:S(2)}) copy-start(f32[2048,64]{1,0:T(8,128)} %gather_fusion) | copy-start | bytes 1572868
  69.6 69.6 %copy-start.4 = (f32[64,64]{1,0:T(8,128)S(1)}, f32[64,64]{1,0:T(8,128)}, u32[]{:S(2)}) copy-start(f32[64,64]{1,0:T(8,128)} %fusion.34) | copy-start | bytes 49156
  77.0 65.5 %copy-start.9 = (f32[3,8,256]{2,1,0:T(8,128)S(1)}, f32[3,8,256]{2,1,0:T(8,128)}, u32[]{:S(2)}) copy-start(f32[3,8,256]{2,1,0:T(8,128)} %get-tuple-element.58) | copy-start | bytes 73732
  77.0 65.5 %copy-start.1 = (f32[64,3,8,256]{3,0,2,1:T(8,128)S(1)}, f32[64,3,8,256]{3,0,2,1:T(8,128)}, u32[]{:S(2)}) copy-start(f32[64,3,8,256]{3,0,2,1:T(8,128)} %get-tuple-element.59) | copy-start | bytes 4718596
where the time goes:
time: 148 us
  blocking collectives  59.5 us (40%)
  local copies, waits for them, and re-layouts  33.2 us (22%)
  starting transfers between devices  23 us (16%)
  other arithmetic  13.7 us (9%)
  matrix products  11.9 us (8%)
  waiting for transfers between devices  5.19 us (4%)
    psum x1, blocking collectives, local(): gram, pull = lax.psum((gram_part, pull_part), ('gx', 'gy'))  59.5 us
    ppermute x4, starting transfers between devices, padded_2(): lax.ppermute(tail, axis, [(i, (i + 1) % count) for i in range(ends)])  13.5 us
    ppermute x4, starting transfers between devices, padded_2(): lax.ppermute(head, axis, [((i + 1) % count, i) for i in range(ends)])  9.47 us
    gather x1, local copies, waits for them, and re-layouts, local(): observed = jnp.take(flat_state, obs_index, axis=1)  7.62 us
    mul x5, local copies, waits for them, and re-layouts, advance(): mixing[:, source][None, :, None, None] * center[:, source][:, None]  7.33 us
    dot_general x1, matrix products, local(): gram_part = jnp.dot(spread, spread.T, precision=lax.Precision.HIGHEST)  5.4 us
    add x1, other arithmetic, advance(): return center + kappa_field[None] * (beside - 4.0 * center) + coupled  4.97 us
    reduce_sum x1, other arithmetic, local(): state_mean = jnp.mean(second_state, axis=0)  4.63 us
  transfers between devices with their start and end apart: 8, of which 3 were waited for; matrix products, arithmetic and copies ran while one was open for 8% of the time, Pallas kernels for 0%

commit v1 on v0

--- a/solution.py
+++ b/solution.py
@@ -76,7 +76,7 @@
     departure = weight * (obs_value[0, 0] - obs_mean)
     gram_part = jnp.dot(spread, spread.T, precision=lax.Precision.HIGHEST)
     pull_part = jnp.dot(spread, departure, precision=lax.Precision.HIGHEST)
-    gram, pull = lax.psum((gram_part, pull_part), ("gx", "gy"))
+    gram, pull = lax.psum(lax.psum((gram_part, pull_part), "gy"), "gx")
     state_mean = jnp.mean(second_state, axis=0)
     anomalies = (second_state - state_mean).reshape(members, -1)
     weights = transform(gram, pull)

time: 148 us -> 120 us (0.81)
  blocking collectives: 59.5 us -> 30.3 us
    psum x1 -> x2, blocking collectives: 59.5 us -> 30.3 us  [local(): gram, pull = lax.psum(lax.psum((gram_part, pull_part), 'gy'), 'gx')]
  transfers between devices with their start and end apart: 8 -> 8, of which waited for: 3 -> 3; matrix products, arithmetic and copies ran while one was open for 8% -> 10% of each run, Pallas kernels for 0% -> 0%
where the time goes in v1:
time: 120 us; the launch traced here: 119 us
  local copies, waits for them, and re-layouts  33.3 us (28%)
  blocking collectives  30.3 us (25%)
  starting transfers between devices  23 us (19%)
  other arithmetic  13.7 us (11%)
  matrix products  11.9 us (10%)
  waiting for transfers between devices  5.23 us (4%)
  between operations  1.21 us (1%)
    psum x2, blocking collectives, local(): gram, pull = lax.psum(lax.psum((gram_part, pull_part), 'gy'), 'gx')  30.3 us
    ppermute x4, starting transfers between devices, padded_2(): lax.ppermute(tail, axis, [(i, (i + 1) % count) for i in range(ends)])  13.5 us
    ppermute x4, starting transfers between devices, padded_2(): lax.ppermute(head, axis, [((i + 1) % count, i) for i in range(ends)])  9.47 us
    gather x1, local copies, waits for them, and re-layouts, local(): observed = jnp.take(flat_state, obs_index, axis=1)  7.61 us
    mul x5, local copies, waits for them, and re-layouts, advance(): mixing[:, source][None, :, None, None] * center[:, source][:, None]  7.33 us
    dot_general x1, matrix products, local(): gram_part = jnp.dot(spread, spread.T, precision=lax.Precision.HIGHEST)  5.4 us
    add x1, other arithmetic, advance(): return center + kappa_field[None] * (beside - 4.0 * center) + coupled  4.94 us
    reduce_sum x1, other arithmetic, local(): state_mean = jnp.mean(second_state, axis=0)  4.64 us
  transfers between devices with their start and end apart: 8, of which 3 were waited for; matrix products, arithmetic and copies ran while one was open for 10% of the time, Pallas kernels for 0%

profile of v1, /device:TPU:2, one launch (start us, length us, event | category | flops | bytes accessed | tf_op | source)
XLA Modules:
  0.0 118.9 jit_solution(3716605879104398254)
XLA Ops:
  0.0 2.0 %copy.48 = f32[64,3,8,256]{3,0,2,1:T(8,128)S(1)} copy(f32[64,3,8,256]{3,2,1,0:T(8,128)} %param.9) | data formatting | bytes 3145728 | tf_op args[0]
  2.1 1.9 %collective-permute-start.1 = (f32[64,3,1,256]{3,0,2,1:T(8,128)S(1)}, f32[64,3,1,256]{3,0,2,1:T(8,128)S(1)}, u32[]{:S(2)}, u32[]{:S(2)}) collective-permute-start(f32[64,3,1,256]{3,0,2,1:T(8,128)S(1)} %get-tuple-element.75), channel_id=1, source_target_pairs={{0,4},{4,8},{8,12},{1,5},{5,9},{9,13},{2,6},{6,10},{10,14},{3,7},{... | collective-permute-start | bytes 589832 | tf_op jit(solution)/shard_map/ppermute | solution.py:18
  4.0 3.6 %collective-permute-start = (f32[64,3,1,256]{3,0,2,1:T(8,128)S(1)}, f32[64,3,1,256]{3,0,2,1:T(8,128)S(1)}, u32[]{:S(2)}, u32[]{:S(2)}) collective-permute-start(f32[64,3,1,256]{3,0,2,1:T(8,128)S(1)} %get-tuple-element.74), channel_id=1, source_target_pairs={{4,0},{8,4},{12,8},{5,1},{9,5},{13,9},{6,2},{10,6},{14,10},{7,3},{... | collective-permute-start | bytes 589832 | tf_op jit(solution)/shard_map/ppermute | solution.py:20
  7.7 1.1 slice_bitcast_fusion.5
  8.8 0.6 fusion.34
  9.5 0.5 constant_dynamic-update-slice_fusion.1
  10.1 0.7 collective-permute-done
  10.9 1.3 %fusion.44 = (f32[64,3,10,1]{3,0,2,1:T(8,128)}, f32[64,3,10,1]{3,0,2,1:T(8,128)S(1)}) fusion(f32[64,3,10,256]{3,0,2,1:T(8,128)S(1)} %constant_dynamic-update-slice_fusion), kind=kLoop, calls=%fused_computation.87 | loop fusion | bytes 30720 | tf_op jit(solution)/shard_map/slice | solution.py:14
  12.2 1.6 %copy.43 = f32[64,3,10,1]{0,3,2,1:T(1,128)S(1)} copy(f32[64,3,10,1]{3,0,2,1:T(8,128)} %get-tuple-element.64) | data formatting | bytes 15360 | tf_op jit(solution)/shard_map/slice | solution.py:14
  13.7 1.3 %collective-permute-start.2 = (f32[64,3,10,1]{0,3,2,1:T(1,128)S(1)}, f32[64,3,10,1]{0,3,2,1:T(1,128)S(1)}, u32[]{:S(2)}, u32[]{:S(2)}) collective-permute-start(f32[64,3,10,1]{0,3,2,1:T(1,128)S(1)} %copy.43), channel_id=1, source_target_pairs={{1,0},{2,1},{3,2},{5,4},{6,5},{7,6},{9,8},{10,9},{11,10},{13,12},{... | collective-permute-start | bytes 23048 | tf_op jit(solution)/shard_map/ppermute | solution.py:20
  15.0 0.3 copy.45
  15.4 4.6 %collective-permute-start.3 = (f32[64,3,10,1]{0,3,2,1:T(1,128)S(1)}, f32[64,3,10,1]{0,3,2,1:T(1,128)S(1)}, u32[]{:S(2)}, u32[]{:S(2)}) collective-permute-start(f32[64,3,10,1]{0,3,2,1:T(1,128)S(1)} %copy.45), channel_id=1, source_target_pairs={{0,1},{1,2},{2,3},{4,5},{5,6},{6,7},{8,9},{9,10},{10,11},{12,13},{... | collective-permute-start | bytes 23048 | tf_op jit(solution)/shard_map/ppermute | solution.py:18
  19.9 0.8 slice_reduce_fusion.2
  20.7 2.0 %copy.49 = f32[64,8,256]{2,0,1:T(8,128)} copy(f32[64,8,256]{2,1,0:T(8,128)} %get-tuple-element.71) | data formatting | bytes 1048576 | tf_op jit(solution)/shard_map/mul | solution.py:33
  22.7 2.0 %copy.50 = f32[64,8,256]{2,0,1:T(8,128)} copy(f32[64,8,256]{2,1,0:T(8,128)} %get-tuple-element.73) | data formatting | bytes 1048576 | tf_op jit(solution)/shard_map/mul | solution.py:33
  24.8 1.0 copy.51
  25.7 1.3 %copy.44 = f32[64,3,10,1]{3,0,2,1:T(8,128)} copy(f32[64,3,10,1]{0,3,2,1:T(1,128)S(1)} %collective-permute-done.2) | data formatting | bytes 15360 | tf_op jit(solution)/shard_map/ppermute | solution.py:20
  27.1 1.3 %copy.46 = f32[64,3,10,1]{3,0,2,1:T(8,128)} copy(f32[64,3,10,1]{0,3,2,1:T(1,128)S(1)} %collective-permute-done.3) | data formatting | bytes 15360 | tf_op jit(solution)/shard_map/ppermute | solution.py:18
  28.4 4.9 %fusion.14 = f32[64,3,8,256]{3,0,2,1:T(8,128)S(1)} fusion(f32[64,3,8,256]{3,0,2,1:T(8,128)} %copy-done.2, f32[64,3,10,256]{3,0,2,1:T(8,128)S(1)} %constant_dynamic-update-slice_fusion, f32[64,3,10,1]{3,0,2,1:T(8,128)} %copy.46, f32[64,3,10,1]{3,0,2,1:T(8,128)} %copy.44, f32[64,3,1,256]{3,0,2,1:T(8,128)} %copy-done.5, f32[64,3,1,256]{3,0,2,1:T(8,128)} %copy-done.6, ...), kind=kLoop, calls=%fused_computation.27 | loop fusion | flops 6684672 | bytes 7117860 | tf_op jit(solution)/shard_map/add | solution.py:34
  33.4 3.3 %collective-permute-start.4 = (f32[64,3,1,256]{3,0,2,1:T(8,128)S(1)}, f32[64,3,1,256]{3,0,2,1:T(8,128)S(1)}, u32[]{:S(2)}, u32[]{:S(2)}) collective-permute-start(f32[64,3,1,256]{3,0,2,1:T(8,128)S(1)} %get-tuple-element.67), channel_id=1, source_target_pairs={{4,0},{8,4},{12,8},{5,1},{9,5},{13,9},{6,2},{10,6},{14,10},{7,3},{... | collective-permute-start | bytes 589832 | tf_op jit(solution)/shard_map/ppermute | solution.py:20
  36.7 1.9 %collective-permute-start.5 = (f32[64,3,1,256]{3,0,2,1:T(8,128)S(1)}, f32[64,3,1,256]{3,0,2,1:T(8,128)S(1)}, u32[]{:S(2)}, u32[]{:S(2)}) collective-permute-start(f32[64,3,1,256]{3,0,2,1:T(8,128)S(1)} %get-tuple-element.66), channel_id=1, source_target_pairs={{0,4},{4,8},{8,12},{1,5},{5,9},{9,13},{2,6},{6,10},{10,14},{3,7},{... | collective-permute-start | bytes 589832 | tf_op jit(solution)/shard_map/ppermute | solution.py:18
  38.6 0.6 compare_and_fusion
  39.2 0.7 collective-permute-done.4
  39.8 3.8 %collective-permute-done.5 = f32[64,3,1,256]{3,0,2,1:T(8,128)S(1)} collective-permute-done((f32[64,3,1,256]{3,0,2,1:T(8,128)S(1)}, f32[64,3,1,256]{3,0,2,1:T(8,128)S(1)}, u32[]{:S(2)}, u32[]{:S(2)}) %collective-permute-start.5) | collective-permute-done | bytes 196640 | tf_op jit(solution)/shard_map/ppermute | solution.py:18
  43.8 0.5 copy-done.8
  44.3 0.4 fusion.43
  44.7 1.0 copy.52
  45.7 1.3 %collective-permute-start.6 = (f32[64,3,10,1]{0,3,2,1:T(1,128)}, f32[64,3,10,1]{0,3,2,1:T(1,128)S(1)}, u32[]{:S(2)}, u32[]{:S(2)}) collective-permute-start(f32[64,3,10,1]{0,3,2,1:T(1,128)} %copy.52), channel_id=1, source_target_pairs={{1,0},{2,1},{3,2},{5,4},{6,5},{7,6},{9,8},{10,9},{11,10},{13,12},{... | collective-permute-start | bytes 23048 | tf_op jit(solution)/shard_map/ppermute | solution.py:20
  46.9 0.3 copy.54
  47.3 5.1 %collective-permute-start.7 = (f32[64,3,10,1]{0,3,2,1:T(1,128)S(1)}, f32[64,3,10,1]{0,3,2,1:T(1,128)}, u32[]{:S(2)}, u32[]{:S(2)}) collective-permute-start(f32[64,3,10,1]{0,3,2,1:T(1,128)S(1)} %copy.54), channel_id=1, source_target_pairs={{0,1},{1,2},{2,3},{4,5},{5,6},{6,7},{8,9},{9,10},{10,11},{12,13},{... | collective-permute-start | bytes 23048 | tf_op jit(solution)/shard_map/ppermute | solution.py:18
  52.4 1.2 %slice_bitcast_fusion.2 = (f32[64,8,256]{2,0,1:T(8,128)}, f32[64,8,256]{2,0,1:T(8,128)}, f32[64,8,256]{2,0,1:T(8,128)}) fusion(f32[64,3,8,256]{3,0,2,1:T(8,128)S(1)} %fusion.14), kind=kLoop, calls=%fused_computation.45 | loop fusion | bytes 3145728 | tf_op jit(solution)/shard_map/mul | solution.py:33
  53.7 0.4 copy.53
  54.1 1.1 copy.55
  55.2 4.6 %fusion.41 = (f32[3,8,256]{2,1,0:T(8,128)}, f32[64,3,8,256]{3,0,2,1:T(8,128)}) fusion(f32[64,8,256]{2,0,1:T(8,128)} %get-tuple-element.70, f32[3]{0:T(128)S(1)} %copy-done.17, f32[64,8,256]{2,0,1:T(8,128)} %get-tuple-element.69, f32[3]{0:T(128)} %get-tuple-element.47, f32[64,8,256]{2,0,1:T(8,128)} %get-tuple-element.68, f32[3]{0:T(128)S(1)} %copy-done.16, ...), kind=kLoop, calls=%fused_computation.85 | loop fusion | flops 8644608 | bytes 5176356 | tf_op jit(solution)/shard_map/reduce_sum | solution.py:80
  59.8 2.1 %copy.64 = f32[64,3,8,256]{0,3,2,1:T(8,128)S(1)} copy(f32[64,3,8,256]{3,0,2,1:T(8,128)} %get-tuple-element.61) | data formatting | bytes 3145728 | tf_op jit(solution)/shard_map/reshape | solution.py:68
  62.0 7.6 %gather_fusion = f32[2048,64]{1,0:T(8,128)} fusion(f32[64,6144]{0,1:T(8,128)S(1)} %bitcast.68, s32[2048]{0:T(1024)S(1)} %broadcast_clamp_fusion), kind=kCustom, calls=%fused_computation | custom fusion | bytes 1056768 | tf_op jit(solution)/shard_map/jit(_take)/gather | solution.py:70
  69.6 1.9 %select_reduce_fusion = f32[2048]{0:T(1024)S(1)} fusion(f32[2048,64]{1,0:T(8,128)} %gather_fusion, pred[2048]{0:T(1024)(128)(4,1)S(1)} %copy-done.11), kind=kLoop, calls=%fused_computation.40 | loop fusion | flops 260096 | bytes 534528 | tf_op jit(solution)/shard_map/reduce_sum | solution.py:71
  71.6 5.4 %fusion.23 = f32[64,64]{1,0:T(8,128)S(1)} fusion(f32[2048,64]{1,0:T(8,128)} %gather_fusion, f32[2048]{0:T(1024)S(1)} %get-tuple-element.78, f32[2048]{0:T(1024)S(1)} %get-tuple-element.77, pred[2048]{0:T(1024)(128)(4,1)S(1)} %copy-done.11), kind=kOutput, calls=%fused_computation.41 | convolution fusion | flops 101056512 | bytes 559104 | tf_op jit(solution)/shard_map/dot_general | solution.py:77
  77.0 1.3 %convolution_bitcast_fusion.1 = f32[64]{0:T(128)S(1)} fusion(f32[2048,1]{0,1:T(1,128)S(1)} %bitcast.75, f32[2048,64]{1,0:T(8,128)S(1)} %copy-done.3, f32[2048]{0:T(1024)S(1)} %get-tuple-element.78, f32[2048]{0:T(1024)S(1)} %get-tuple-element.77, pred[2048]{0:T(1024)(128)(4,1)S(1)} %copy-done.11), kind=kOutput, calls=%fused_computation.36 | convolution fusion | flops 1966080 | bytes 551168 | tf_op jit(solution)/shard_map/dot_general | solution.py:78
  78.3 19.6 %all-reduce = (f32[64,64]{1,0:T(8,128)S(1)}, f32[64]{0:T(128)S(1)}) all-reduce(f32[64,64]{1,0:T(8,128)S(1)} %fusion.23, f32[64]{0:T(128)S(1)} %convolution_bitcast_fusion.1), channel_id=1, replica_groups=mesh['grp'=2,'gx'=4,'gy'=4] {'gy'}, use_global_device_ids=true, to_apply=%region_2.3 | all-reduce | flops 4160 | bytes 33280 | tf_op jit(solution)/shard_map/psum | solution.py:79
  98.0 10.7 %all-reduce.1 = (f32[64,64]{1,0:T(8,128)S(1)}, f32[64]{0:T(128)S(1)}) all-reduce(f32[64,64]{1,0:T(8,128)S(1)} %get-tuple-element.54, f32[64]{0:T(128)S(1)} %get-tuple-element.55), channel_id=1, replica_groups=mesh['grp'=2,'gx'=4,'gy'=4] {'gx'}, use_global_device_ids=true, to_apply=%region_3.4 | all-reduce | flops 4160 | bytes 33280 | tf_op jit(solution)/shard_map/psum | solution.py:79
  108.6 0.7 multiply_reduce_fusion
  110.2 3.2 %while.13 = (s32[]{:T(128)}, f32[64,64]{0,1:T(8,128)S(1)}, f32[64,64]{1,0:T(8,128)S(1)}, s32[]{:T(128)}) while((s32[]{:T(128)}, f32[64,64]{0,1:T(8,128)S(1)}, f32[64,64]{1,0:T(8,128)S(1)}, s32[]{:T(128)}) %tuple.41), condition=%wide.region_6.7_spmd.clone, body=%wide.region_5.6_spmd.clone.sunk | while | flops 9453570 | bytes 213045 | solution.py:56
  110.6 0.2 convolution_bitcast_fusion.4
  111.2 0.2 convolution_bitcast_fusion.4
  113.6 0.9 copy.68
  114.8 1.9 %fusion.19 = f32[64,3,8,256]{3,0,2,1:T(8,128)S(1)} fusion(f32[3,8,256,64]{2,1,0,3:T(8,128)S(1)} %bitcast.69, f32[3,8,256]{2,1,0:T(8,128)S(1)} %broadcast_multiply_fusion, f32[64]{0:T(128)S(1)} %convolution_bitcast_fusion.2, f32[64,64]{1,0:T(8,128)S(1)} %get-tuple-element.27, f32[]{:T(128)S(6)} %sqrt.7), kind=kOutput, calls=%fused_computation.35 | convolution fusion | flops 302391296 | bytes 3186948 | tf_op jit(solution)/shard_map/dot_general | solution.py:83
  116.8 2.1 %copy.62 = f32[64,3,8,256]{3,2,1,0:T(8,128)} copy(f32[64,3,8,256]{3,0,2,1:T(8,128)S(1)} %fusion.19) | data formatting | bytes 3145728 | tf_op jit(solution)/shard_map/add | solution.py:84
  (77 shorter events, 3.5 us)
Async XLA Ops:
  0.0 7.7 %copy-start = (f32[64,3,8,256]{3,2,1,0:T(8,128)S(1)}, f32[64,3,8,256]{3,2,1,0:T(8,128)}, u32[]{:S(2)}) copy-start(f32[64,3,8,256]{3,2,1,0:T(8,128)} %param.9) | copy-start | bytes 4718596
  2.0 6.8 %copy-start.2 = (f32[64,3,8,256]{3,0,2,1:T(8,128)}, f32[64,3,8,256]{3,0,2,1:T(8,128)S(1)}, u32[]{:S(2)}) copy-start(f32[64,3,8,256]{3,0,2,1:T(8,128)S(1)} %copy.48) | copy-start | bytes 4718596
  2.1 7.4 %collective-permute-start.1 = (f32[64,3,1,256]{3,0,2,1:T(8,128)S(1)}, f32[64,3,1,256]{3,0,2,1:T(8,128)S(1)}, u32[]{:S(2)}, u32[]{:S(2)}) collective-permute-start(f32[64,3,1,256]{3,0,2,1:T(8,128)S(1)} %get-tuple-element.75), channel_id=1, source_target_pairs={{0,4},{4,8},{8,12},{1,5},{5,9},{9,13},{2,6},{6,10},{10,14},{3,7},{... | collective-permute-start | bytes 589832 | tf_op jit(solution)/shard_map/ppermute | solution.py:18
  4.0 5.4 %copy-start.12 = (s32[1,1,2048]{2,1,0:T(1,128)S(1)}, s32[1,1,2048]{2,1,0:T(1,128)}, u32[]{:S(2)}) copy-start(s32[1,1,2048]{2,1,0:T(1,128)} %param.12) | copy-start | bytes 24580
  4.0 5.4 %copy-start.13 = (s32[1,1,2048]{2,1,0:T(1,128)S(1)}, s32[1,1,2048]{2,1,0:T(1,128)}, u32[]{:S(2)}) copy-start(s32[1,1,2048]{2,1,0:T(1,128)} %param.13) | copy-start | bytes 24580
  4.0 6.8 %collective-permute-start = (f32[64,3,1,256]{3,0,2,1:T(8,128)S(1)}, f32[64,3,1,256]{3,0,2,1:T(8,128)S(1)}, u32[]{:S(2)}, u32[]{:S(2)}) collective-permute-start(f32[64,3,1,256]{3,0,2,1:T(8,128)S(1)} %get-tuple-element.74), channel_id=1, source_target_pairs={{4,0},{8,4},{12,8},{5,1},{9,5},{13,9},{6,2},{10,6},{14,10},{7,3},{... | collective-permute-start | bytes 589832 | tf_op jit(solution)/shard_map/ppermute | solution.py:20
  9.5 0.7 copy-start.5
  10.9 1.3 %copy-start.6 = (f32[64,3,1,256]{3,0,2,1:T(8,128)}, f32[64,3,1,256]{3,0,2,1:T(8,128)S(1)}, u32[]{:S(2)}) copy-start(f32[64,3,1,256]{3,0,2,1:T(8,128)S(1)} %collective-permute-done) | copy-start | bytes 589828
  12.2 7.8 %copy-start.10 = (f32[3,3]{1,0:T(4,128)S(1)}, f32[3,3]{1,0:T(4,128)}, u32[]{:S(2)}) copy-start(f32[3,3]{1,0:T(4,128)} %param.11) | copy-start | bytes 112
  13.7 12.0 %collective-permute-start.2 = (f32[64,3,10,1]{0,3,2,1:T(1,128)S(1)}, f32[64,3,10,1]{0,3,2,1:T(1,128)S(1)}, u32[]{:S(2)}, u32[]{:S(2)}) collective-permute-start(f32[64,3,10,1]{0,3,2,1:T(1,128)S(1)} %copy.43), channel_id=1, source_target_pairs={{1,0},{2,1},{3,2},{5,4},{6,5},{7,6},{9,8},{10,9},{11,10},{13,12},{... | collective-permute-start | bytes 23048 | tf_op jit(solution)/shard_map/ppermute | solution.py:20
  15.4 11.7 %collective-permute-start.3 = (f32[64,3,10,1]{0,3,2,1:T(1,128)S(1)}, f32[64,3,10,1]{0,3,2,1:T(1,128)S(1)}, u32[]{:S(2)}, u32[]{:S(2)}) collective-permute-start(f32[64,3,10,1]{0,3,2,1:T(1,128)S(1)} %copy.45), channel_id=1, source_target_pairs={{0,1},{1,2},{2,3},{4,5},{5,6},{6,7},{8,9},{9,10},{10,11},{12,13},{... | collective-permute-start | bytes 23048 | tf_op jit(solution)/shard_map/ppermute | solution.py:18
  33.4 6.4 %collective-permute-start.4 = (f32[64,3,1,256]{3,0,2,1:T(8,128)S(1)}, f32[64,3,1,256]{3,0,2,1:T(8,128)S(1)}, u32[]{:S(2)}, u32[]{:S(2)}) collective-permute-start(f32[64,3,1,256]{3,0,2,1:T(8,128)S(1)} %get-tuple-element.67), channel_id=1, source_target_pairs={{4,0},{8,4},{12,8},{5,1},{9,5},{13,9},{6,2},{10,6},{14,10},{7,3},{... | collective-permute-start | bytes 589832 | tf_op jit(solution)/shard_map/ppermute | solution.py:20
  36.7 7.0 %collective-permute-start.5 = (f32[64,3,1,256]{3,0,2,1:T(8,128)S(1)}, f32[64,3,1,256]{3,0,2,1:T(8,128)S(1)}, u32[]{:S(2)}, u32[]{:S(2)}) collective-permute-start(f32[64,3,1,256]{3,0,2,1:T(8,128)S(1)} %get-tuple-element.66), channel_id=1, source_target_pairs={{0,4},{4,8},{8,12},{1,5},{5,9},{9,13},{2,6},{6,10},{10,14},{3,7},{... | collective-permute-start | bytes 589832 | tf_op jit(solution)/shard_map/ppermute | solution.py:18
  39.8 4.0 %copy-start.7 = (f32[64,3,1,256]{3,0,2,1:T(8,128)}, f32[64,3,1,256]{3,0,2,1:T(8,128)S(1)}, u32[]{:S(2)}) copy-start(f32[64,3,1,256]{3,0,2,1:T(8,128)S(1)} %collective-permute-done.4) | copy-start | bytes 589828
  43.7 0.7 copy-start.8
  45.7 8.0 %collective-permute-start.6 = (f32[64,3,10,1]{0,3,2,1:T(1,128)}, f32[64,3,10,1]{0,3,2,1:T(1,128)S(1)}, u32[]{:S(2)}, u32[]{:S(2)}) collective-permute-start(f32[64,3,10,1]{0,3,2,1:T(1,128)} %copy.52), channel_id=1, source_target_pairs={{1,0},{2,1},{3,2},{5,4},{6,5},{7,6},{9,8},{10,9},{11,10},{13,12},{... | collective-permute-start | bytes 23048 | tf_op jit(solution)/shard_map/ppermute | solution.py:20
  47.3 6.8 %collective-permute-start.7 = (f32[64,3,10,1]{0,3,2,1:T(1,128)S(1)}, f32[64,3,10,1]{0,3,2,1:T(1,128)}, u32[]{:S(2)}, u32[]{:S(2)}) collective-permute-start(f32[64,3,10,1]{0,3,2,1:T(1,128)S(1)} %copy.54), channel_id=1, source_target_pairs={{0,1},{1,2},{2,3},{4,5},{5,6},{6,7},{8,9},{9,10},{10,11},{12,13},{... | collective-permute-start | bytes 23048 | tf_op jit(solution)/shard_map/ppermute | solution.py:18
  53.7 1.5 %copy-start.16 = (f32[3]{0:T(128)S(1)}, f32[3]{0:T(128)}, u32[]{:S(2)}) copy-start(f32[3]{0:T(128)} %get-tuple-element.45) | copy-start | bytes 40
  53.7 1.5 %copy-start.17 = (f32[3]{0:T(128)S(1)}, f32[3]{0:T(128)}, u32[]{:S(2)}) copy-start(f32[3]{0:T(128)} %get-tuple-element.46) | copy-start | bytes 40
  61.9 7.6 %copy-start.11 = (pred[2048]{0:T(1024)(128)(4,1)S(1)}, pred[2048]{0:T(1024)(128)(4,1)}, u32[]{:S(2)}) copy-start(pred[2048]{0:T(1024)(128)(4,1)} %compare_and_fusion) | copy-start | bytes 6148
  61.9 9.6 %copy-start.14 = (f32[1,1,2048]{2,1,0:T(1,128)S(1)}, f32[1,1,2048]{2,1,0:T(1,128)}, u32[]{:S(2)}) copy-start(f32[1,1,2048]{2,1,0:T(1,128)} %param.15) | copy-start | bytes 24580
  62.0 9.6 %copy-start.15 = (f32[1,1,2048]{2,1,0:T(1,128)S(1)}, f32[1,1,2048]{2,1,0:T(1,128)}, u32[]{:S(2)}) copy-start(f32[1,1,2048]{2,1,0:T(1,128)} %param.14) | copy-start | bytes 24580
  69.6 7.4 %copy-start.3 = (f32[2048,64]{1,0:T(8,128)S(1)}, f32[2048,64]{1,0:T(8,128)}, u32[]{:S(2)}) copy-start(f32[2048,64]{1,0:T(8,128)} %gather_fusion) | copy-start | bytes 1572868
  69.6 40.6 %copy-start.4 = (f32[64,64]{1,0:T(8,128)S(1)}, f32[64,64]{1,0:T(8,128)}, u32[]{:S(2)}) copy-start(f32[64,64]{1,0:T(8,128)} %fusion.34) | copy-start | bytes 49156
  77.0 36.5 %copy-start.9 = (f32[3,8,256]{2,1,0:T(8,128)S(1)}, f32[3,8,256]{2,1,0:T(8,128)}, u32[]{:S(2)}) copy-start(f32[3,8,256]{2,1,0:T(8,128)} %get-tuple-element.60) | copy-start | bytes 73732
  77.0 36.5 %copy-start.1 = (f32[64,3,8,256]{3,0,2,1:T(8,128)S(1)}, f32[64,3,8,256]{3,0,2,1:T(8,128)}, u32[]{:S(2)}) copy-start(f32[64,3,8,256]{3,0,2,1:T(8,128)} %get-tuple-element.61) | copy-start | bytes 4718596
